TPU v7x, 128 devices: a whole 4x4x4 slice. The times are simulated.
128 devices in a mesh: row: 4 (over x), col: 8 (over z_lo, y), layer: 4 (over z_hi, core).
Axes of the slice: x: 4, y: 4, z: 4 (z_hi: 2, z_lo: 2; z = z_hi * 2 + z_lo), core: 2. Of those that a mesh axis runs over, the one named last changes fastest.
Arguments:
- a_blocks: float32 [4096, 4096], P('row', ('col', 'layer')), may hold values from -6 to 6
- mask_a: int32 [64, 64], P('row', ('col', 'layer')), may hold values from 0 to 1, as said below
- b_blocks: float32 [4096, 32768], P('row', ('col', 'layer')), may hold values from -0.25 to 0.25
- mask_b: int32 [64, 512], P('row', ('col', 'layer')), may hold values from 0 to 1
Outputs:
- product: float32 [4096, 32768], P('row', ('col', 'layer'))
Inputs may be any that keep to these rules, and one draw needn't show every extreme that they name: Within one device's shard of mask_a (16 block rows by 2 inner block indices) at most 8 blocks are stored; the shard of the first 16 block rows and first 2 inner indices stores exactly 8.
All inputs are finite; a program needn't handle non-finite values.
Results may differ from a plain program's by a relative error of at most 0.00007.
Values sent between devices are 32-bit elements; how exact they have to be, the bound alone decides.
No kernel may reach another device: no remote copies, remote signals or barrier semaphores. Data moves between devices by JAX's collectives and lax.ppermute only.
A program may use at most 128 MiB of HBM per device.

v0:
```python
import jax
import jax.numpy as jnp
from jax import lax
from jax.sharding import PartitionSpec as P

BLOCK = 64


def expand(mask):
    return jnp.repeat(jnp.repeat(mask, BLOCK, axis=0), BLOCK, axis=1).astype(jnp.float32)


def shards(a_blocks, mask_a, b_blocks, mask_b):
    b_masked = b_blocks * expand(mask_b)
    b_whole = lax.all_gather(b_masked, "row", axis=0, tiled=True)
    a_masked = a_blocks * expand(mask_a)
    return jnp.dot(
        lax.all_gather(a_masked, ("col", "layer"), axis=1, tiled=True),
        b_whole,
        precision=lax.Precision.HIGHEST,
        preferred_element_type=jnp.float32,
    )


def solution(mesh):
    placed = (
        P("row", ("col", "layer")),
        P("row", ("col", "layer")),
        P("row", ("col", "layer")),
        P("row", ("col", "layer")),
    )
    return jax.shard_map(
        shards, mesh=mesh, in_specs=placed, out_specs=P("row", ("col", "layer")), check_vma=False
    )
```

profile of v0, /device:TPU:1, one launch (start us, length us, event | category | flops | bytes accessed | tf_op | source)
XLA Modules:
  0.0 392.4 jit_solution(702926884030204920)
XLA Ops:
  6.5 0.0 copy-start
  6.5 0.0 copy-start.1
  6.5 0.0 all-gather.5.cloned.1.call-start
  6.5 5.4 %copy.8 = f32[1024,1024]{0,1:T(8,128)} copy(f32[1024,1024]{1,0:T(8,128)} %param.6) | data formatting | bytes 8388608 | tf_op args[2]
  11.9 0.7 convert_element_type.25
  12.6 0.1 copy.7
  12.7 0.1 broadcast_in_dim.14
  12.8 0.1 convert_element_type.26
  12.9 5.1 %bitcast_multiply_fusion = f32[1024,1024]{0,1:T(8,128)} fusion(f32[1024,1024]{0,1:T(8,128)} %copy.8, f32[1024,16]{0,1:T(8,128)S(1)} %convert_element_type.26), kind=kLoop, calls=%fused_computation | loop fusion | flops 1048576 | bytes 8454144 | tf_op jit(solution)/shard_map/mul | solution.py:14
  18.0 0.0 all-gather.5.cloned.1.call-update
  18.0 0.0 all-gather.3.cloned.1.call-start
  18.0 0.0 copy-done
  18.1 0.2 copy.6
  18.3 0.0 copy-done.1
  18.3 0.1 broadcast_in_dim.12
  18.4 0.1 convert_element_type.23
  18.4 0.9 bitcast_multiply_fusion.1
  19.3 0.0 all-gather.3.cloned.1.call-update
  19.3 156.1 %all-gather.5.cloned.1.call-done = f32[4096,1024]{0,1:T(8,128)} async-done(((f32[1024,1024]{0,1:T(8,128)}), f32[4096,1024]{0,1:T(8,128)}) %all-gather.5.cloned.1.call-update) | async-done | bytes 16777232 | tf_op jit(solution)/shard_map/all_gather | solution.py:15
  175.4 100.4 %all-gather.3.cloned.1.call-done = f32[1024,4096]{0,1:T(8,128)} async-done(((f32[1024,128]{0,1:T(8,128)}), f32[1024,4096]{0,1:T(8,128)}) %all-gather.3.cloned.1.call-update) | async-done | bytes 16777232 | tf_op jit(solution)/shard_map/all_gather | solution.py:18
  275.8 109.8 %fusion = f32[1024,1024]{1,0:T(8,128)} fusion(f32[1024,4096]{0,1:T(8,128)} %all-gather.3.cloned.1.call-done, f32[4096,1024]{0,1:T(8,128)} %all-gather.5.cloned.1.call-done), kind=kOutput, calls=%fused_computation.2 | convolution fusion | flops 51539607552 | bytes 37748736 | tf_op jit(solution)/shard_map/dot_general | solution.py:17
  (1 shorter events, 0.0 us)
Async XLA Ops:
  6.5 11.5 %copy-start = (f32[1024,128]{1,0:T(8,128)S(1)}, f32[1024,128]{1,0:T(8,128)}, u32[]{:S(2)}) copy-start(f32[1024,128]{1,0:T(8,128)} %param.4) | copy-start | bytes 1572868
  6.5 11.7 %copy-start.1 = (s32[16,2]{0,1:T(2,128)S(1)}, s32[16,2]{0,1:T(2,128)}, u32[]{:S(2)}) copy-start(s32[16,2]{0,1:T(2,128)} %param.5) | copy-start | bytes 388
  6.5 168.9 %all-gather.5.cloned.1.call-start = ((), (), s32[]{:S(2)}) async-start(), calls=%async_computation.1 | async-start | bytes 20971520 | tf_op jit(solution)/shard_map/all_gather | solution.py:15
  18.0 257.8 %all-gather.3.cloned.1.call-start = ((), (), s32[]{:S(2)}) async-start(), calls=%async_computation | async-start | bytes 17301504 | tf_op jit(solution)/shard_map/all_gather | solution.py:18
Sparse Core Ops, SparseCore 0:
  18.1 157.2 all-gather.4
  177.1 98.6 all-gather.2
where the time goes:
time: 393 us; the launch traced here: 392 us
  waiting for transfers between devices  256 us (65%)
  matrix products  110 us (28%)
  between operations  13.4 us (3%)
  other arithmetic  6.62 us (2%)
  local copies, waits for them, and re-layouts  6.02 us (2%)
    all_gather x1, waiting for transfers between devices, shards(): b_whole = lax.all_gather(b_masked, 'row', axis=0, tiled=True)  156 us
    dot_general x1, matrix products, shards(): jnp.dot(lax.all_gather(a_masked, ('col', 'layer'), axis=1, tiled=True), b...  110 us
    all_gather x1, waiting for transfers between devices, shards(): lax.all_gather(a_masked, ('col', 'layer'), axis=1, tiled=True)  100 us
  transfers between devices with their start and end apart: 2, of which 2 were waited for; matrix products, arithmetic and copies ran while one was open for 0% of the time, Pallas kernels for 0%

commit v1 on v0

--- a/solution.py
+++ b/solution.py
@@ -12,7 +12,9 @@
 
 def shards(a_blocks, mask_a, b_blocks, mask_b):
     b_masked = b_blocks * expand(mask_b)
-    b_whole = lax.all_gather(b_masked, "row", axis=0, tiled=True)
+    b_whole = jnp.concatenate(
+        lax.all_to_all(jnp.stack([b_masked] * lax.axis_size("row")), "row", 0, 0), axis=0
+    )
     a_masked = a_blocks * expand(mask_a)
     return jnp.dot(
         lax.all_gather(a_masked, ("col", "layer"), axis=1, tiled=True),

time: 393 us -> 299 us (0.76)
  waiting for transfers between devices: 256 us -> 0.02 us
  blocking collectives: 0 us -> 195 us
  matrix products: 110 us -> 59.5 us
  local copies, waits for them, and re-layouts: 6.02 us -> 23 us
    all_to_all x0 -> x1, blocking collectives: none -> 195 us  [shards(): lax.all_to_all(jnp.stack([b_masked] * lax.axis_size('row')), 'row', 0, 0)]
    all_gather x1 -> x0, waiting for transfers between devices: 156 us -> none  [shards(): b_whole = lax.all_gather(b_masked, 'row', axis=0, tiled=True)]
    all_gather x1, waiting for transfers between devices: 100 us -> 0.01 us  [shards(): lax.all_gather(a_masked, ('col', 'layer'), axis=1, tiled=True)]
    dot_general x1, matrix products: 110 us -> 59.5 us  [shards(): jnp.dot(lax.all_gather(a_masked, ('col', 'layer'), axis=1, tiled=True), b...]
    another operation x0 -> x1, local copies, waits for them, and re-layouts: none -> 10.6 us  [shards(): jnp.stack([b_masked] * lax.axis_size('row'))]
    mul x0 -> x1, local copies, waits for them, and re-layouts: none -> 5.42 us  [shards(): b_masked = b_blocks * expand(mask_b)]
  transfers between devices with their start and end apart: 2 -> 1, of which waited for: 2 -> 0; matrix products, arithmetic and copies ran while one was open for 0% -> 9% of each run, Pallas kernels for 0% -> 0%
where the time goes in v1:
time: 299 us
  blocking collectives  195 us (65%)
  matrix products  59.5 us (20%)
  local copies, waits for them, and re-layouts  23 us (8%)
  between operations  13.4 us (4%)
  other arithmetic  7.3 us (2%)
    all_to_all x1, blocking collectives, shards(): lax.all_to_all(jnp.stack([b_masked] * lax.axis_size('row')), 'row', 0, 0)  195 us
    dot_general x1, matrix products, shards(): jnp.dot(lax.all_gather(a_masked, ('col', 'layer'), axis=1, tiled=True), b...  59.5 us
    another operation x1, local copies, waits for them, and re-layouts, shards(): jnp.stack([b_masked] * lax.axis_size('row'))  10.6 us
    unnamed x2, local copies, waits for them, and re-layouts  6.58 us
  transfers between devices with their start and end apart: 1, of which 0 were waited for; matrix products, arithmetic and copies ran while one was open for 9% of the time, Pallas kernels for 0%

profile of v1, /device:TPU:1, one launch (start us, length us, event | category | flops | bytes accessed | tf_op | source)
XLA Modules:
  0.0 298.6 jit_solution(2731565274236527439)
XLA Ops:
  6.5 0.0 all-gather.2.cloned.1.call-start
  6.5 1.2 copy.6
  7.8 0.7 convert_element_type.22
  8.5 0.1 broadcast_in_dim.12
  8.5 0.1 convert_element_type.23
  8.6 0.9 bitcast_multiply_fusion.1
  9.5 0.0 all-gather.2.cloned.1.call-update
  9.5 5.3 %copy.8 = f32[1024,1024]{0,1:T(8,128)} copy(f32[1024,1024]{1,0:T(8,128)} %param.6) | data formatting | bytes 8388608 | tf_op args[2]
  14.9 0.7 convert_element_type.25
  15.5 0.1 copy.7
  15.6 0.1 broadcast_in_dim.14
  15.7 0.1 convert_element_type.26
  15.8 5.1 %bitcast_multiply_fusion = f32[1024,1024]{0,1:T(8,128)} fusion(f32[1024,1024]{0,1:T(8,128)} %copy.8, f32[1024,16]{0,1:T(8,128)S(1)} %convert_element_type.26), kind=kLoop, calls=%fused_computation | loop fusion | flops 1048576 | bytes 8454144 | tf_op jit(solution)/shard_map/mul | solution.py:14
  20.9 5.4 %copy.9 = f32[1024,1024]{1,0:T(8,128)} copy(f32[1024,1024]{0,1:T(8,128)} %bitcast_multiply_fusion) | data formatting | bytes 8388608 | tf_op jit(solution)/shard_map/mul | solution.py:14
  26.3 10.6 %stack.2 = f32[4,1024,1024]{2,1,0:T(8,128)} broadcast(f32[1024,1024]{1,0:T(8,128)} %copy.9), dimensions={1,2} | broadcast | bytes 20971520 | tf_op jit(solution)/shard_map/stack | solution.py:16
  36.9 195.3 %all_to_all.5 = f32[4,1024,1024]{2,1,0:T(8,128)} all-to-all(f32[4,1024,1024]{2,1,0:T(8,128)} %stack.2), channel_id=1, replica_groups=mesh['row'=4,'col'=8,'layer'=4] {'row'}, dimensions={0} | all-to-all | bytes 33554432 | tf_op jit(solution)/shard_map/all_to_all | solution.py:16
  232.2 0.0 all-gather.2.cloned.1.call-done
  232.3 59.5 %fusion = f32[1024,1024]{1,0:T(8,128)} fusion(f32[1024,4096]{0,1:T(8,128)} %all-gather.2.cloned.1.call-done, f32[4096,1024]{1,0:T(8,128)} %bitcast.11), kind=kOutput, calls=%fused_computation.2 | convolution fusion | flops 51539607552 | bytes 37748736 | tf_op jit(solution)/shard_map/dot_general | solution.py:19
Async XLA Ops:
  6.5 225.7 %all-gather.2.cloned.1.call-start = ((), (), s32[]{:S(2)}) async-start(), calls=%async_computation.1 | async-start | bytes 17301504 | tf_op jit(solution)/shard_map/all_gather | solution.py:20
Sparse Core Ops, SparseCore 0:
  9.6 100.8 all-gather.1
